TPU v7x, 256 devices: a whole 4x4x8 slice. The times are simulated.
256 devices in a mesh: region: 8 (over x, core), dom: 32 (over z, y).
Axes of the slice: x: 4, y: 4, z: 8, core: 2. Of those that a mesh axis runs over, the one named last changes fastest.
Arguments:
- x_init: bfloat16 [1048576, 128], P(('region', 'dom')), may hold values from -6 to 6
- tiles: bfloat16 [73728, 128, 128], P(('region', 'dom'))
- tile_row: int32 [73728], P(('region', 'dom')), may hold values from 0 to 31
- tile_col: int32 [73728], P(('region', 'dom')), may hold values from 0 to 63, as said below
- send_list: int32 [256, 4, 8], P(('region', 'dom')), may hold values from 0 to 31, as said below
- send_count: int32 [256, 4], P(('region', 'dom')), may hold values from 1 to 8, as said below
Outputs:
- basis: bfloat16 [1048576, 128], P(('region', 'dom'))
- ritz_matrix: float32 [2, 128, 128], replicated
Inputs may be any that keep to these rules, and one draw needn't show every extreme that they name: `send_list`: the 8 entries of one partition and direction are distinct row tiles of that partition. `send_count`: some partition sends 8 row tiles in every direction. `tile_col`: a value 32 + d * 8 + s with d = 0 .. 3 names slot s of the d-th received stack of extended, and s is below the count that this neighbour sends; no value names a stack where the neighbour does not exist.
All inputs are finite; a program needn't handle non-finite values.
Results may differ from a plain program's by a relative error of at most 0.00115.
The roundings to bfloat16 on the way count: a program that leaves them out, or rounds other values in their place, can miss the bound.
Values may be sent and summed in bfloat16 or wider, within the bound.
No kernel may reach another device: no remote copies, remote signals or barrier semaphores. Data moves between devices by JAX's collectives and lax.ppermute only.
A program may use at most 64 MiB of HBM per device.

v0:
```python
import math
import jax
import jax.numpy as jnp
from jax import lax
from jax.sharding import PartitionSpec as P

ITERS = 2
HIGH = lax.Precision.HIGHEST


def shifted(block, axis, distance):
    devices = range(lax.axis_size(axis))
    route = [(i - distance, i) for i in devices if i - distance in devices]
    return lax.ppermute(block, axis, route)


def local_gram(current, node_total):
    return (
        lax.dot_general(
            current, current, (((0,), (0,)), ((), ())), preferred_element_type=jnp.float32
        )
        / node_total
    )


def rayleigh_sum(partial_value):
    return lax.psum(partial_value, ("region", "dom"))


def pass_dom(packed, offset):
    return shifted(packed, "dom", offset)


def pass_region(packed, offset):
    return shifted(packed, "region", offset)


def apply_graph(basis, tiles, tile_row, tile_col, send_rows, live_slot, row_tiles, tile_size):
    vectors = basis.shape[1]
    blocks = basis.reshape(row_tiles, tile_size, vectors)
    picked = blocks[send_rows]
    packed = jnp.where(live_slot[:, :, None, None], picked, jnp.zeros_like(picked))
    received = [
        pass_dom(packed[0], 1),
        pass_dom(packed[1], -1),
        pass_region(packed[2], 1),
        pass_region(packed[3], -1),
    ]
    extended = jnp.concatenate([blocks] + received, axis=0)
    group = 32
    group_count = tiles.shape[0] // group
    tile_groups = tiles.reshape(group_count, group, tile_size, tile_size)
    col_groups = tile_col.reshape(group_count, group)
    row_groups = tile_row.reshape(group_count, group)
    row_ids = jnp.arange(row_tiles, dtype=jnp.int32)

    def add_group(accumulated, pieces):
        tile_part, col_part, row_part = pieces
        gathered = extended[col_part]
        products = lax.dot_general(
            tile_part, gathered, (((2,), (1,)), ((0,), (0,))), preferred_element_type=jnp.float32
        )
        select = (row_part[None, :] == row_ids[:, None]).astype(jnp.float32)
        return (accumulated + jnp.einsum("rt,tiw->riw", select, products, precision=HIGH), None)

    start = jnp.zeros((row_tiles, tile_size, vectors), jnp.float32)
    applied, _ = lax.scan(add_group, start, (tile_groups, col_groups, row_groups))
    return applied.reshape(row_tiles * tile_size, vectors)


def shards(x_init, tiles, tile_row, tile_col, send_list, send_count):
    row_count, vectors = x_init.shape
    tile_size = tiles.shape[1]
    row_tiles = row_count // tile_size
    capacity = send_list.shape[2]
    node_total = row_count * lax.axis_size("region") * lax.axis_size("dom")
    root_total = math.sqrt(node_total)
    send_rows = send_list[0]
    live_slot = jnp.arange(capacity, dtype=jnp.int32)[None, :] < send_count[0][:, None]
    identity = jnp.eye(vectors, dtype=jnp.float32)
    current = x_init
    gram = lax.psum(local_gram(current, node_total), ("region", "dom"))
    rayleigh_list = []
    basis = x_init
    for iteration in range(ITERS):
        factor = jnp.linalg.cholesky(gram)
        inverse = lax.linalg.triangular_solve(factor, identity, left_side=True, lower=True)
        basis = jnp.dot(current.astype(jnp.float32), inverse.T, precision=HIGH).astype(jnp.bfloat16)
        applied = apply_graph(
            basis, tiles, tile_row, tile_col, send_rows, live_slot, row_tiles, tile_size
        )
        partial_value = jnp.dot(basis.astype(jnp.float32).T, applied, precision=HIGH) / root_total
        if iteration + 1 < ITERS:
            current = applied.astype(jnp.bfloat16)
            rayleigh_list.append(rayleigh_sum(partial_value))
            gram = lax.psum(local_gram(current, node_total), ("region", "dom"))
        else:
            rayleigh_list.append(rayleigh_sum(partial_value))
    return (basis, jnp.stack(rayleigh_list))


def solution(mesh):
    in_specs = (
        P(("region", "dom"), None),
        P(("region", "dom"), None, None),
        P(("region", "dom")),
        P(("region", "dom")),
        P(("region", "dom"), None, None),
        P(("region", "dom"), None),
    )
    out_specs = (P(("region", "dom"), None), P())
    return jax.shard_map(shards, mesh=mesh, in_specs=in_specs, out_specs=out_specs, check_vma=False)
```

profile of v0, /device:TPU:2, one launch (start us, length us, event | category | flops | bytes accessed | tf_op | source)
XLA Modules:
  0.0 1021.1 jit_solution(12112515196211047036)
XLA Ops:
  9.8 247.8 %all-reduce.5.cloned.1.call-done = f32[128,128]{0,1:T(8,128)} async-done(((f32[128,128]{0,1:T(8,128)}), f32[128,128]{0,1:T(8,128)}) %all-reduce.5.cloned.1.call-update) | async-done | bytes 65552 | tf_op jit(solution)/shard_map/psum | solution.py:82
  259.4 11.7 %cholesky.44 = f32[128,128]{1,0:T(8,128)S(1)} custom-call(f32[128,128]{1,0:T(8,128)S(1)} %fusion.46), custom_call_target="Cholesky" | custom-call | tf_op jit(solution)/shard_map/jit(cholesky)/cholesky | solution.py:86
  272.4 9.8 custom-call.8
  288.2 3.0 collective-permute-start
  292.6 2.4 collective-permute-start.2
  295.1 3.3 collective-permute-start.3
  298.5 3.4 collective-permute-done.1
  303.6 82.5 %while.22 = (s32[]{:T(128)}, f32[32,128,128]{2,0,1:T(8,128)}, s32[9,32]{1,0:T(8,128)S(1)}, bf16[9,32,128,128]{3,2,1,0:T(8,128)(2,1)}, s32[9,32]{1,0:T(8,128)S(1)...) while((s32[]{:T(128)}, f32[32,128,128]{2,0,1:T(8,128)}, s32[9,32]{1,0:T(8,128)S(1)}, ...), condition=%wide.region_4.7_spmd.clone, body=%wide.region_3.6_spmd.clone.sunk | while | flops 336595040 | bytes 29365292 | solution.py:67
  303.6 2.3 gather_fusion
  307.8 3.5 select_add_fusion.4
  312.8 2.3 gather_fusion
  317.0 3.5 select_add_fusion.4
  321.9 2.3 gather_fusion
  324.3 1.8 fusion.77
  326.2 3.5 select_add_fusion.4
  331.1 2.3 gather_fusion
  333.5 1.8 fusion.77
  335.4 3.5 select_add_fusion.4
  340.3 2.3 gather_fusion
  342.6 1.8 fusion.77
  344.5 3.5 select_add_fusion.4
  349.4 2.3 gather_fusion
  353.7 3.5 select_add_fusion.4
  358.6 2.3 gather_fusion
  361.0 1.8 fusion.77
  362.9 3.5 select_add_fusion.4
  367.8 2.3 gather_fusion
  372.0 3.5 select_add_fusion.4
  376.9 2.3 gather_fusion
  379.3 1.8 fusion.77
  381.2 3.5 select_add_fusion.4
  386.1 3.5 fusion.32
  389.6 2.6 copy.20
  392.2 239.2 %all-reduce.7.cloned.1.call-done = f32[128,128]{0,1:T(8,128)} async-done(((f32[128,128]{0,1:T(8,128)}), f32[128,128]{0,1:T(8,128)}) %all-reduce.7.cloned.1.call-update) | async-done | bytes 65552 | tf_op jit(solution)/shard_map/psum | solution.py:96
  633.2 11.7 %cholesky.55 = f32[128,128]{1,0:T(8,128)S(1)} custom-call(f32[128,128]{1,0:T(8,128)S(1)} %fusion.44), custom_call_target="Cholesky" | custom-call | tf_op jit(solution)/shard_map/jit(cholesky)/cholesky | solution.py:86
  646.3 9.8 custom-call.9
  656.4 2.6 convolution_convert_fusion
  661.5 4.6 collective-permute-start.4
  666.0 1.9 fusion.34
  667.9 1.9 collective-permute-start.6
  670.0 3.9 collective-permute-start.7
  675.7 1.8 collective-permute-done.7
  678.8 82.3 %while.23 = (s32[]{:T(128)}, f32[32,128,128]{2,0,1:T(8,128)}, s32[9,32]{1,0:T(8,128)S(1)}, bf16[9,32,128,128]{3,2,1,0:T(8,128)(2,1)}, s32[9,32]{1,0:T(8,128)S(1)...) while((s32[]{:T(128)}, f32[32,128,128]{2,0,1:T(8,128)}, s32[9,32]{1,0:T(8,128)S(1)}, ...), condition=%wide.region_8.11_spmd.clone, body=%wide.region_7.10_spmd.clone.sunk | while | flops 336595040 | bytes 29365292 | solution.py:67
  678.8 2.3 gather_fusion.1
  683.1 3.5 select_add_fusion.5
  688.0 2.3 gather_fusion.1
  692.2 3.5 select_add_fusion.5
  697.1 2.3 gather_fusion.1
  701.4 3.5 select_add_fusion.5
  706.3 2.3 gather_fusion.1
  710.5 3.5 select_add_fusion.5
  715.4 2.3 gather_fusion.1
  719.7 3.5 select_add_fusion.5
  724.6 2.3 gather_fusion.1
  728.8 3.5 select_add_fusion.5
  733.7 2.3 gather_fusion.1
  738.0 3.5 select_add_fusion.5
  742.9 2.3 gather_fusion.1
  747.1 3.5 select_add_fusion.5
  752.0 2.3 gather_fusion.1
  756.3 3.5 select_add_fusion.5
  761.1 2.8 copy.25
  763.9 2.0 fusion.33
  766.0 247.0 %all-reduce.9.cloned.1.call-done = (f32[1,128,128]{2,1,0:T(8,128)}, f32[1,128,128]{2,1,0:T(8,128)}) async-done(((f32[1,128,128]{2,1,0:T(8,128)}, f32[1,128,128]{2,1,0:T(8,128)}), (f32[1,128,128]{2,1,0:T(8,128)}, f32[1,128,128]{2,1,0:T(8,128)})) %all-reduce.9.cloned.1.call-update) | async-done | bytes 131088 | tf_op jit(solution)/shard_map/psum | solution.py:27
  (217 shorter events, 74.9 us)
Async XLA Ops:
  7.2 1.2 copy-start
  7.2 2.4 copy-start.15
  7.2 2.5 copy-start.14
  7.2 250.4 %all-reduce.5.cloned.1.call-start = ((), (), s32[]{:S(2)}) async-start(), calls=%async_computation | async-start | bytes 131072 | tf_op jit(solution)/shard_map/psum | solution.py:82
  9.5 621.9 %all-reduce.7.cloned.1.call-start = ((), (), s32[]{:S(2)}) async-start(), calls=%async_computation.1 | async-start | bytes 131072 | tf_op jit(solution)/shard_map/psum | solution.py:96
  283.5 2.3 copy-start.10
  285.9 6.6 copy-start.12
  285.9 6.7 copy-start.13
  288.2 10.3 %collective-permute-start = (bf16[8,128,128]{2,1,0:T(8,128)(2,1)}, bf16[8,128,128]{2,1,0:T(8,128)(2,1)S(1)}, u32[]{:S(2)}, u32[]{:S(2)}) collective-permute-start(bf16[8,128,128]{2,1,0:T(8,128)(2,1)} %get-tuple-element.159), channel_id=1, source_target_pairs={{0,1},{1,2},{2,3},{3,4},{4,5},{5,6},{6,7},{7,8},{8,9},{9,10},{10,1... | collective-permute-start | bytes 786440 | tf_op jit(solution)/shard_map/ppermute | solution.py:14
  291.2 10.8 %collective-permute-start.1 = (bf16[8,128,128]{2,1,0:T(8,128)(2,1)}, bf16[8,128,128]{2,1,0:T(8,128)(2,1)S(1)}, u32[]{:S(2)}, u32[]{:S(2)}) collective-permute-start(bf16[8,128,128]{2,1,0:T(8,128)(2,1)} %get-tuple-element.158), channel_id=1, source_target_pairs={{1,0},{2,1},{3,2},{4,3},{5,4},{6,5},{7,6},{8,7},{9,8},{10,9},{11,1... | collective-permute-start | bytes 786440 | tf_op jit(solution)/shard_map/ppermute | solution.py:14
  292.6 9.4 collective-permute-start.2
  295.1 7.0 collective-permute-start.3
  302.2 1.3 copy-start.6
  305.9 1.9 copy-start.1
  311.4 1.4 copy-start.2
  315.1 1.9 copy-start.1
  320.5 1.4 copy-start.2
  324.3 1.9 copy-start.1
  329.7 1.4 copy-start.2
  333.4 1.9 copy-start.1
  338.9 1.4 copy-start.2
  342.6 1.9 copy-start.1
  348.0 1.4 copy-start.2
  351.8 1.9 copy-start.1
  357.2 1.4 copy-start.2
  360.9 1.9 copy-start.1
  366.4 1.4 copy-start.2
  370.1 1.9 copy-start.1
  375.5 1.4 copy-start.2
  379.3 1.9 copy-start.1
  384.7 1.4 copy-start.2
  386.1 3.6 copy-start.3
  389.6 623.4 %all-reduce.9.cloned.1.call-start = ((), (), s32[]{:S(2)}) async-start(), calls=%async_computation.2 | async-start | bytes 262144 | tf_op jit(solution)/shard_map/psum | solution.py:27
  659.0 105.0 %copy-start.9 = (bf16[4096,128]{1,0:T(8,128)(2,1)}, bf16[4096,128]{1,0:T(8,128)(2,1)S(1)}, u32[]{:S(2)}) copy-start(bf16[4096,128]{1,0:T(8,128)(2,1)S(1)} %convolution_convert_fusion) | copy-start | bytes 3145732
  659.7 6.3 copy-start.8
  659.8 6.3 copy-start.11
  660.0 13.9 %collective-permute-start.5 = (bf16[8,128,128]{2,1,0:T(8,128)(2,1)S(1)}, bf16[8,128,128]{2,1,0:T(8,128)(2,1)S(1)}, u32[]{:S(2)}, u32[]{:S(2)}) collective-permute-start(bf16[8,128,128]{2,1,0:T(8,128)(2,1)S(1)} %get-tuple-element.154), channel_id=1, source_target_pairs={{1,0},{2,1},{3,2},{4,3},{5,4},{6,5},{7,6},{8,7},{9,8},{10,9},{11,1... | collective-permute-start | bytes 786440 | tf_op jit(solution)/shard_map/ppermute | solution.py:14
  661.5 12.4 %collective-permute-start.4 = (bf16[8,128,128]{2,1,0:T(8,128)(2,1)S(1)}, bf16[8,128,128]{2,1,0:T(8,128)(2,1)S(1)}, u32[]{:S(2)}, u32[]{:S(2)}) collective-permute-start(bf16[8,128,128]{2,1,0:T(8,128)(2,1)S(1)} %get-tuple-element.155), channel_id=1, source_target_pairs={{0,1},{1,2},{2,3},{3,4},{4,5},{5,6},{6,7},{7,8},{8,9},{9,10},{10,1... | collective-permute-start | bytes 786440 | tf_op jit(solution)/shard_map/ppermute | solution.py:14
  667.9 7.7 collective-permute-start.6
  670.0 7.5 collective-permute-start.7
  677.5 1.3 copy-start.7
  681.2 1.9 copy-start.4
  686.6 1.3 copy-start.5
  690.3 1.9 copy-start.4
  695.8 1.3 copy-start.5
  699.5 1.9 copy-start.4
  704.9 1.3 copy-start.5
  708.6 1.9 copy-start.4
  714.1 1.3 copy-start.5
  717.8 1.9 copy-start.4
  723.2 1.3 copy-start.5
  726.9 1.9 copy-start.4
  732.3 1.3 copy-start.5
  736.1 1.9 copy-start.4
  741.5 1.3 copy-start.5
  745.2 1.9 copy-start.4
  750.6 1.3 copy-start.5
  754.4 1.9 copy-start.4
  759.8 1.3 copy-start.5
Sparse Core Ops, SparseCore 0:
  14.1 243.4 all-reduce.4
  389.7 241.6 all-reduce.6
  766.1 246.8 all-reduce.8
where the time goes:
time: 1020 us
  waiting for transfers between devices  741 us (73%)
  matrix products  108 us (11%)
  local copies, waits for them, and re-layouts  83.8 us (8%)
  other arithmetic  50.8 us (5%)
  starting transfers between devices  21.9 us (2%)
  between operations  14.2 us (1%)
    psum x2, waiting for transfers between devices, shards(): gram = lax.psum(local_gram(current, node_total), ('region', 'dom'))  487 us
    psum x1, waiting for transfers between devices, rayleigh_sum(): return lax.psum(partial_value, ('region', 'dom'))  247 us
    dot_general x18, matrix products, add_group(): jnp.einsum('rt,tiw->riw', select, products, precision=HIGH)  63.3 us
    gather x18, local copies, waits for them, and re-layouts, add_group(): gathered = extended[col_part]  42.1 us
    dot_general x18, matrix products, add_group(): lax.dot_general(tile_part, gathered, (((2,), (1,)), ((0,), (0,))), prefer...  32.4 us
    while x72, local copies, waits for them, and re-layouts  25.8 us
    another operation x6, other arithmetic, shards(): factor = jnp.linalg.cholesky(gram)  24.8 us
    ppermute x8, starting transfers between devices, shifted(): return lax.ppermute(block, axis, route)  21.8 us
  transfers between devices with their start and end apart: 11, of which 7 were waited for; matrix products, arithmetic and copies ran while one was open for 1% of the time, Pallas kernels for 0%

commit v1 on v0

--- a/solution.py
+++ b/solution.py
@@ -24,7 +24,8 @@
 
 
 def rayleigh_sum(partial_value):
-    return lax.psum(partial_value, ("region", "dom"))
+    set_signs = lambda which_axis, mesh_ax, packet: lax.psum(lax.psum(packet, mesh_ax), which_axis)
+    return set_signs("region", "dom", partial_value)
 
 
 def pass_dom(packed, offset):

time: 1020 us -> 985 us (0.966)
  waiting for transfers between devices: 741 us -> 701 us
    psum x1 -> x2, waiting for transfers between devices: 247 us -> 207 us  [the longest x1 144 us: rayleigh_sum(): lax.psum(packet, mesh_ax)]
  transfers between devices with their start and end apart: 11 -> 12, of which waited for: 7 -> 8; matrix products, arithmetic and copies ran while one was open for 1% -> 1% of each run, Pallas kernels for 0% -> 0%
where the time goes in v1:
time: 985 us; the launch traced here: 981 us
  waiting for transfers between devices  701 us (71%)
  matrix products  108 us (11%)
  local copies, waits for them, and re-layouts  83.8 us (9%)
  other arithmetic  50.8 us (5%)
  starting transfers between devices  21.9 us (2%)
  between operations  14.2 us (1%)
    psum x2, waiting for transfers between devices, shards(): gram = lax.psum(local_gram(current, node_total), ('region', 'dom'))  487 us
    psum x1, waiting for transfers between devices, rayleigh_sum(): lax.psum(packet, mesh_ax)  144 us
    psum x1, waiting for transfers between devices, rayleigh_sum(): lax.psum(lax.psum(packet, mesh_ax), which_axis)  63.6 us
    dot_general x18, matrix products, add_group(): jnp.einsum('rt,tiw->riw', select, products, precision=HIGH)  63.3 us
    gather x18, local copies, waits for them, and re-layouts, add_group(): gathered = extended[col_part]  42.1 us
    dot_general x18, matrix products, add_group(): lax.dot_general(tile_part, gathered, (((2,), (1,)), ((0,), (0,))), prefer...  32.4 us
    while x72, local copies, waits for them, and re-layouts  25.8 us
    another operation x6, other arithmetic, shards(): factor = jnp.linalg.cholesky(gram)  24.8 us
  transfers between devices with their start and end apart: 12, of which 8 were waited for; matrix products, arithmetic and copies ran while one was open for 1% of the time, Pallas kernels for 0%

profile of v1, /device:TPU:2, one launch (start us, length us, event | category | flops | bytes accessed | tf_op | source)
XLA Modules:
  0.0 981.4 jit_solution(18150699073633119909)
XLA Ops:
  9.8 247.8 %all-reduce.7.cloned.1.call-done = f32[128,128]{0,1:T(8,128)} async-done(((f32[128,128]{0,1:T(8,128)}), f32[128,128]{0,1:T(8,128)}) %all-reduce.7.cloned.1.call-update) | async-done | bytes 65552 | tf_op jit(solution)/shard_map/psum | solution.py:83
  259.4 11.7 %cholesky.44 = f32[128,128]{1,0:T(8,128)S(1)} custom-call(f32[128,128]{1,0:T(8,128)S(1)} %fusion.44), custom_call_target="Cholesky" | custom-call | tf_op jit(solution)/shard_map/jit(cholesky)/cholesky | solution.py:87
  272.4 9.8 custom-call.8
  288.2 3.0 collective-permute-start
  292.6 2.4 collective-permute-start.2
  295.1 3.3 collective-permute-start.3
  298.5 3.4 collective-permute-done.1
  303.5 82.5 %while.22 = (s32[]{:T(128)}, f32[32,128,128]{2,0,1:T(8,128)}, s32[9,32]{1,0:T(8,128)S(1)}, bf16[9,32,128,128]{3,2,1,0:T(8,128)(2,1)}, s32[9,32]{1,0:T(8,128)S(1)...) while((s32[]{:T(128)}, f32[32,128,128]{2,0,1:T(8,128)}, s32[9,32]{1,0:T(8,128)S(1)}, ...), condition=%wide.region_4.7_spmd.clone, body=%wide.region_3.6_spmd.clone.sunk | while | flops 336595040 | bytes 29365292 | solution.py:68
  303.6 2.3 gather_fusion
  307.8 3.5 select_add_fusion.4
  312.7 2.3 gather_fusion
  315.1 1.8 fusion.75
  317.0 3.5 select_add_fusion.4
  321.9 2.3 gather_fusion
  326.2 3.5 select_add_fusion.4
  331.1 2.3 gather_fusion
  333.4 1.8 fusion.75
  335.3 3.5 select_add_fusion.4
  340.2 2.3 gather_fusion
  344.5 3.5 select_add_fusion.4
  349.4 2.3 gather_fusion
  353.7 3.5 select_add_fusion.4
  358.6 2.3 gather_fusion
  360.9 1.8 fusion.75
  362.8 3.5 select_add_fusion.4
  367.7 2.3 gather_fusion
  372.0 3.5 select_add_fusion.4
  376.9 2.3 gather_fusion
  381.2 3.5 select_add_fusion.4
  386.1 3.5 fusion.32
  389.6 2.6 copy.20
  392.2 239.2 %all-reduce.9.cloned.1.call-done = f32[128,128]{0,1:T(8,128)} async-done(((f32[128,128]{0,1:T(8,128)}), f32[128,128]{0,1:T(8,128)}) %all-reduce.9.cloned.1.call-update) | async-done | bytes 65552 | tf_op jit(solution)/shard_map/psum | solution.py:97
  633.2 11.7 %cholesky.55 = f32[128,128]{1,0:T(8,128)S(1)} custom-call(f32[128,128]{1,0:T(8,128)S(1)} %fusion.42), custom_call_target="Cholesky" | custom-call | tf_op jit(solution)/shard_map/jit(cholesky)/cholesky | solution.py:87
  646.3 9.8 custom-call.9
  656.4 2.6 convolution_convert_fusion
  661.5 4.6 collective-permute-start.4
  666.1 1.9 convolution_multiply_fusion.2
  667.9 1.9 collective-permute-start.6
  670.0 3.9 collective-permute-start.7
  675.7 1.8 collective-permute-done.7
  678.8 82.3 %while.23 = (s32[]{:T(128)}, f32[32,128,128]{2,0,1:T(8,128)}, s32[9,32]{1,0:T(8,128)S(1)}, bf16[9,32,128,128]{3,2,1,0:T(8,128)(2,1)}, s32[9,32]{1,0:T(8,128)S(1)...) while((s32[]{:T(128)}, f32[32,128,128]{2,0,1:T(8,128)}, s32[9,32]{1,0:T(8,128)S(1)}, ...), condition=%wide.region_9.12_spmd.clone, body=%wide.region_8.11_spmd.clone.sunk | while | flops 336595040 | bytes 29365292 | solution.py:68
  678.9 2.3 gather_fusion.1
  683.1 3.5 select_add_fusion.5
  688.0 2.3 gather_fusion.1
  692.3 3.5 select_add_fusion.5
  697.2 2.3 gather_fusion.1
  701.4 3.5 select_add_fusion.5
  706.3 2.3 gather_fusion.1
  710.6 3.5 select_add_fusion.5
  715.4 2.3 gather_fusion.1
  717.8 1.8 fusion.82
  719.7 3.5 select_add_fusion.5
  724.6 2.3 gather_fusion.1
  728.8 3.5 select_add_fusion.5
  733.7 2.3 gather_fusion.1
  738.0 3.5 select_add_fusion.5
  742.9 2.3 gather_fusion.1
  747.1 3.5 select_add_fusion.5
  752.0 2.3 gather_fusion.1
  756.3 3.5 select_add_fusion.5
  761.1 2.8 copy.25
  764.0 2.0 convolution_multiply_fusion.1
  766.1 143.6 %all-reduce.11.cloned.1.call-done = (f32[128,128]{1,0:T(8,128)}, f32[128,128]{1,0:T(8,128)}) async-done(((f32[128,128]{1,0:T(8,128)}, f32[128,128]{1,0:T(8,128)}), (f32[128,128]{1,0:T(8,128)}, f32[128,128]{1,0:T(8,128)})) %all-reduce.11.cloned.1.call-update) | async-done | bytes 131088 | tf_op jit(solution)/shard_map/psum | solution.py:27
  909.7 63.6 %all-reduce.13.cloned.1.call-done = (f32[1,128,128]{2,1,0:T(8,128)}, f32[1,128,128]{2,1,0:T(8,128)}) async-done(((f32[1,128,128]{2,1,0:T(8,128)}, f32[1,128,128]{2,1,0:T(8,128)}), (f32[1,128,128]{2,1,0:T(8,128)}, f32[1,128,128]{2,1,0:T(8,128)})) %all-reduce.13.cloned.1.call-update) | async-done | bytes 131088 | tf_op jit(solution)/shard_map/psum | solution.py:27
  (220 shorter events, 76.7 us)
Async XLA Ops:
  7.2 1.2 copy-start
  7.2 2.4 copy-start.15
  7.2 2.5 copy-start.14
  7.2 250.4 %all-reduce.7.cloned.1.call-start = ((), (), s32[]{:S(2)}) async-start(), calls=%async_computation | async-start | bytes 131072 | tf_op jit(solution)/shard_map/psum | solution.py:83
  9.5 621.9 %all-reduce.9.cloned.1.call-start = ((), (), s32[]{:S(2)}) async-start(), calls=%async_computation.1 | async-start | bytes 131072 | tf_op jit(solution)/shard_map/psum | solution.py:97
  283.5 2.3 copy-start.10
  285.9 6.6 copy-start.12
  285.9 6.7 copy-start.13
  288.2 10.3 %collective-permute-start = (bf16[8,128,128]{2,1,0:T(8,128)(2,1)}, bf16[8,128,128]{2,1,0:T(8,128)(2,1)S(1)}, u32[]{:S(2)}, u32[]{:S(2)}) collective-permute-start(bf16[8,128,128]{2,1,0:T(8,128)(2,1)} %get-tuple-element.161), channel_id=1, source_target_pairs={{0,1},{1,2},{2,3},{3,4},{4,5},{5,6},{6,7},{7,8},{8,9},{9,10},{10,1... | collective-permute-start | bytes 786440 | tf_op jit(solution)/shard_map/ppermute | solution.py:14
  291.1 10.8 %collective-permute-start.1 = (bf16[8,128,128]{2,1,0:T(8,128)(2,1)}, bf16[8,128,128]{2,1,0:T(8,128)(2,1)S(1)}, u32[]{:S(2)}, u32[]{:S(2)}) collective-permute-start(bf16[8,128,128]{2,1,0:T(8,128)(2,1)} %get-tuple-element.160), channel_id=1, source_target_pairs={{1,0},{2,1},{3,2},{4,3},{5,4},{6,5},{7,6},{8,7},{9,8},{10,9},{11,1... | collective-permute-start | bytes 786440 | tf_op jit(solution)/shard_map/ppermute | solution.py:14
  292.6 9.4 collective-permute-start.2
  295.1 7.0 collective-permute-start.3
  302.2 1.3 copy-start.6
  305.9 1.9 copy-start.1
  311.4 1.4 copy-start.2
  315.1 1.9 copy-start.1
  320.5 1.4 copy-start.2
  324.3 1.9 copy-start.1
  329.7 1.4 copy-start.2
  333.4 1.9 copy-start.1
  338.9 1.4 copy-start.2
  342.6 1.9 copy-start.1
  348.0 1.4 copy-start.2
  351.8 1.9 copy-start.1
  357.2 1.4 copy-start.2
  360.9 1.9 copy-start.1
  366.4 1.4 copy-start.2
  370.1 1.9 copy-start.1
  375.5 1.4 copy-start.2
  379.3 1.9 copy-start.1
  384.7 1.4 copy-start.2
  386.1 3.6 copy-start.3
  389.6 520.1 %all-reduce.11.cloned.1.call-start = ((), (), s32[]{:S(2)}) async-start(), calls=%async_computation.2 | async-start | bytes 262144 | tf_op jit(solution)/shard_map/psum | solution.py:27
  659.0 105.0 %copy-start.9 = (bf16[4096,128]{1,0:T(8,128)(2,1)}, bf16[4096,128]{1,0:T(8,128)(2,1)S(1)}, u32[]{:S(2)}) copy-start(bf16[4096,128]{1,0:T(8,128)(2,1)S(1)} %convolution_convert_fusion) | copy-start | bytes 3145732
  659.8 6.3 copy-start.8
  659.8 6.3 copy-start.11
  660.0 13.9 %collective-permute-start.5 = (bf16[8,128,128]{2,1,0:T(8,128)(2,1)S(1)}, bf16[8,128,128]{2,1,0:T(8,128)(2,1)S(1)}, u32[]{:S(2)}, u32[]{:S(2)}) collective-permute-start(bf16[8,128,128]{2,1,0:T(8,128)(2,1)S(1)} %get-tuple-element.156), channel_id=1, source_target_pairs={{1,0},{2,1},{3,2},{4,3},{5,4},{6,5},{7,6},{8,7},{9,8},{10,9},{11,1... | collective-permute-start | bytes 786440 | tf_op jit(solution)/shard_map/ppermute | solution.py:14
  661.5 12.4 %collective-permute-start.4 = (bf16[8,128,128]{2,1,0:T(8,128)(2,1)S(1)}, bf16[8,128,128]{2,1,0:T(8,128)(2,1)S(1)}, u32[]{:S(2)}, u32[]{:S(2)}) collective-permute-start(bf16[8,128,128]{2,1,0:T(8,128)(2,1)S(1)} %get-tuple-element.157), channel_id=1, source_target_pairs={{0,1},{1,2},{2,3},{3,4},{4,5},{5,6},{6,7},{7,8},{8,9},{9,10},{10,1... | collective-permute-start | bytes 786440 | tf_op jit(solution)/shard_map/ppermute | solution.py:14
  667.9 7.7 collective-permute-start.6
  670.0 7.5 collective-permute-start.7
  677.5 1.3 copy-start.7
  681.2 1.9 copy-start.4
  686.6 1.3 copy-start.5
  690.4 1.9 copy-start.4
  695.8 1.3 copy-start.5
  699.5 1.9 copy-start.4
  704.9 1.3 copy-start.5
  708.6 1.9 copy-start.4
  714.1 1.3 copy-start.5
  717.8 1.9 copy-start.4
  723.2 1.3 copy-start.5
  726.9 1.9 copy-start.4
  732.4 1.3 copy-start.5
  736.1 1.9 copy-start.4
  741.5 1.3 copy-start.5
  745.2 1.9 copy-start.4
  750.7 1.3 copy-start.5
  754.4 1.9 copy-start.4
  759.8 1.3 copy-start.5
  766.0 207.3 %all-reduce.13.cloned.1.call-start = ((), (), s32[]{:S(2)}) async-start(), calls=%async_computation.3 | async-start | bytes 262144 | tf_op jit(solution)/shard_map/psum | solution.py:27
Sparse Core Ops, SparseCore 0:
  14.1 243.4 all-reduce.6
  389.7 241.7 all-reduce.8
  766.1 143.4 all-reduce.10
  911.9 61.3 all-reduce.12
